TPU v7x, 32 devices: a whole 2x2x4 slice. The times are simulated.
32 devices in a mesh: batch: 16 (over z, y, x), stream: 2 (over core).
Axes of the slice: x: 2, y: 2, z: 4, core: 2. Of those that a mesh axis runs over, the one named last changes fastest.
Arguments:
- tokens: bfloat16 [128, 198, 768], P(('batch', 'stream')), may hold values from -6 to 6
- prompts: float32 [50, 768], replicated, may hold values from -6 to 6
- keep_mask: int32 [128, 196], P(('batch', 'stream')), may hold values from 0 to 1, as said below
- counts: int32 [128], P(('batch', 'stream')), may hold values from 79 to 196, as said below
- ln1_gain: float32 [768], replicated, may hold values from 0.5 to 1.5
- ln1_bias: float32 [768], replicated, may hold values from -0.6 to 0.6
- w_qkv: bfloat16 [768, 2304], replicated, may hold values from -0.21875 to 0.21875
- q_bias: float32 [768], replicated, may hold values from -0.6 to 0.6
- v_bias: float32 [768], replicated, may hold values from -0.6 to 0.6
- w_out: bfloat16 [768, 768], replicated, may hold values from -2.5 to 2.5
- out_bias: float32 [768], replicated, may hold values from -0.6 to 0.6
- ln2_gain: float32 [768], replicated, may hold values from 0.5 to 1.5
- ln2_bias: float32 [768], replicated, may hold values from -0.6 to 0.6
- w_fc1: bfloat16 [768, 3072], replicated, may hold values from -0.21875 to 0.21875
- fc1_bias: float32 [3072], replicated, may hold values from -0.6 to 0.6
- w_fc2: bfloat16 [3072, 768], replicated, may hold values from -0.109375 to 0.109375
- fc2_bias: float32 [768], replicated, may hold values from -0.6 to 0.6
- cot_seq: bfloat16 [128, 198, 768], P(('batch', 'stream')), may hold values from -6 to 6
- cot_prompt: bfloat16 [128, 50, 768], P(('batch', 'stream')), may hold values from -6 to 6
Outputs:
- layer_out: bfloat16 [128, 198, 768], P(('batch', 'stream'))
- prompt_out: bfloat16 [128, 50, 768], P(('batch', 'stream'))
- input_grad: float32 [128, 198, 768], P(('batch', 'stream'))
- prompt_grad: float32 [50, 768], replicated
- penalty: float32 [], replicated
Inputs may be any that keep to these rules, and one draw needn't show every extreme that they name: `keep_mask`: 1 keeps a patch; row i has exactly counts[i] ones. counts[i] is the number of ones in row i of keep_mask.
All inputs are finite; a program needn't handle non-finite values.
Results may differ from a plain program's by a relative error of at most 0.01.
Values sent between devices are 32-bit elements; how exact they have to be, the bound alone decides.
A program may use at most 128 MiB of HBM per device.

v0:
```python
import math
import jax
import jax.numpy as jnp
from jax import lax
from jax.sharding import PartitionSpec as P

HEADS = 12
EPSILON = 1e-06


def layer_norm(values_in, norm_gain, norm_shift):
    row_mean = jnp.mean(values_in, axis=-1, keepdims=True)
    centered = values_in - row_mean
    variance = jnp.mean(centered * centered, axis=-1, keepdims=True)
    return centered * lax.rsqrt(variance + EPSILON) * norm_gain + norm_shift


def split_heads(tensor, head_count):
    return tensor.reshape(
        tensor.shape[0], tensor.shape[1], head_count, tensor.shape[2] // head_count
    )


def masked_scores(queries, key_part, live_keys, head_count, score_scale):
    raw_scores = jnp.einsum(
        "iqhd,ikhd->ihqk",
        split_heads(queries, head_count),
        split_heads(key_part, head_count),
        preferred_element_type=jnp.float32,
    )
    return jnp.where(live_keys[:, None, None, :], raw_scores * score_scale, -1e30)


def project_pairs(pair_grads, pair_weight):
    return jnp.einsum("pe,de->pd", pair_grads, pair_weight, precision=lax.Precision.HIGHEST)


def body(
    tokens,
    prompts,
    keep_mask,
    counts,
    ln1_gain,
    ln1_bias,
    w_qkv,
    q_bias,
    v_bias,
    w_out,
    out_bias,
    ln2_gain,
    ln2_bias,
    w_fc1,
    fc1_bias,
    w_fc2,
    fc2_bias,
    cot_seq,
    cot_prompt,
):
    images, seq_length, model_width = tokens.shape
    prompt_count = prompts.shape[0]
    head_count = HEADS
    score_scale = (model_width // head_count) ** (-0.5)
    total_images = images * lax.axis_size("batch") * lax.axis_size("stream")
    count_sum = jnp.sum(counts.astype(jnp.float32))
    kept_total = lax.psum(count_sum, ("batch", "stream"))
    keep_full = jnp.concatenate(
        [jnp.ones((images, seq_length - keep_mask.shape[1]), jnp.int32), keep_mask], axis=1
    )
    kept_cols = keep_full[:, :, None] > 0
    live_keys = (
        jnp.concatenate([jnp.ones((images, prompt_count), jnp.int32), keep_full], axis=1) > 0
    )
    prompt_normed, prompt_norm_back = jax.vjp(
        lambda rows_in: layer_norm(rows_in, ln1_gain, ln1_bias), prompts
    )
    prompt_proj = jnp.dot(
        prompt_normed.astype(jnp.bfloat16), w_qkv, preferred_element_type=jnp.float32
    )
    prompt_query = (prompt_proj[:, :model_width] + q_bias).astype(jnp.bfloat16)
    prompt_pairs = jnp.concatenate(
        [prompt_proj[:, model_width : 2 * model_width], prompt_proj[:, 2 * model_width :] + v_bias],
        axis=1,
    ).astype(jnp.bfloat16)
    token_rows = tokens.astype(jnp.float32)
    token_normed, token_norm_back = jax.vjp(
        lambda rows_in: layer_norm(rows_in, ln1_gain, ln1_bias), token_rows
    )
    token_proj = jnp.einsum(
        "ihd,de->ihe", token_normed.astype(jnp.bfloat16), w_qkv, preferred_element_type=jnp.float32
    )
    token_query = (token_proj[..., :model_width] + q_bias).astype(jnp.bfloat16)
    token_pairs = jnp.concatenate(
        [
            token_proj[..., model_width : 2 * model_width],
            token_proj[..., 2 * model_width :] + v_bias,
        ],
        axis=2,
    ).astype(jnp.bfloat16)
    queries = jnp.concatenate(
        [jnp.broadcast_to(prompt_query[None], (images, prompt_count, model_width)), token_query],
        axis=1,
    )
    pairs = jnp.concatenate(
        [
            jnp.broadcast_to(prompt_pairs[None], (images, prompt_count, 2 * model_width)),
            token_pairs,
        ],
        axis=1,
    )
    key_part = pairs[..., :model_width]
    value_part = pairs[..., model_width:]
    value_heads = split_heads(value_part, head_count)
    scores = masked_scores(queries, key_part, live_keys, head_count, score_scale)
    top_score = jnp.max(scores, axis=-1, keepdims=True)
    log_total = top_score + jnp.log(jnp.sum(jnp.exp(scores - top_score), axis=-1, keepdims=True))
    soft_low = jnp.exp(scores - log_total).astype(jnp.bfloat16)
    context = jnp.einsum(
        "ihqk,ikhd->iqhd", soft_low, value_heads, preferred_element_type=jnp.float32
    )
    context = context.reshape(images, -1, model_width).astype(jnp.bfloat16)
    attention = (
        jnp.einsum("ird,de->ire", context, w_out, preferred_element_type=jnp.float32) + out_bias
    )
    residual = jnp.concatenate(
        [jnp.broadcast_to(prompts[None], (images, prompt_count, model_width)), token_rows], axis=1
    )
    middle = residual + attention
    second_norm, second_norm_back = jax.vjp(
        lambda rows_in: layer_norm(rows_in, ln2_gain, ln2_bias), middle
    )
    hidden = (
        jnp.einsum(
            "ird,df->irf",
            second_norm.astype(jnp.bfloat16),
            w_fc1,
            preferred_element_type=jnp.float32,
        )
        + fc1_bias
    )
    activated, gelu_back = jax.vjp(lambda rows_in: jax.nn.gelu(rows_in, approximate=False), hidden)
    result = (
        middle
        + jnp.einsum(
            "irf,fd->ird", activated.astype(jnp.bfloat16), w_fc2, preferred_element_type=jnp.float32
        )
        + fc2_bias
    )
    prompt_out = result[:, :prompt_count].astype(jnp.bfloat16)
    layer_out = jnp.where(kept_cols, result[:, prompt_count:], token_rows).astype(jnp.bfloat16)
    grad_result = jnp.concatenate(
        [cot_prompt, jnp.where(kept_cols, cot_seq, jnp.zeros_like(cot_seq))], axis=1
    )
    grad_act = jnp.einsum("ird,fd->irf", grad_result, w_fc2, preferred_element_type=jnp.float32)
    grad_hidden = gelu_back(grad_act)[0].astype(jnp.bfloat16)
    grad_second = jnp.einsum("irf,df->ird", grad_hidden, w_fc1, preferred_element_type=jnp.float32)
    grad_middle = grad_result.astype(jnp.float32) + second_norm_back(grad_second)[0]
    grad_context = jnp.einsum(
        "ire,de->ird", grad_middle.astype(jnp.bfloat16), w_out, preferred_element_type=jnp.float32
    ).astype(jnp.bfloat16)
    again = masked_scores(queries, key_part, live_keys, head_count, score_scale)
    soft_full = jnp.exp(again - log_total)
    soft_back = soft_full.astype(jnp.bfloat16)
    context_heads = split_heads(grad_context, head_count)
    grad_soft = jnp.einsum(
        "iqhd,ikhd->ihqk", context_heads, value_heads, preferred_element_type=jnp.float32
    )
    grad_values = jnp.einsum(
        "ihqk,iqhd->ikhd", soft_back, context_heads, preferred_element_type=jnp.float32
    ).reshape(images, -1, model_width)
    row_dot = jnp.sum(soft_full * grad_soft, axis=-1, keepdims=True)
    grad_scores = (soft_full * (grad_soft - row_dot)).astype(jnp.bfloat16)
    grad_queries = (
        jnp.einsum(
            "ihqk,ikhd->iqhd",
            grad_scores,
            split_heads(key_part, head_count),
            preferred_element_type=jnp.float32,
        )
        * score_scale
    )
    grad_queries = grad_queries.reshape(images, -1, model_width).astype(jnp.bfloat16)
    grad_keys = (
        jnp.einsum(
            "ihqk,iqhd->ikhd",
            grad_scores,
            split_heads(queries, head_count),
            preferred_element_type=jnp.float32,
        )
        * score_scale
    ).reshape(images, -1, model_width)
    grad_pairs = jnp.concatenate([grad_keys, grad_values], axis=2)
    token_proj_grad = jnp.concatenate(
        [grad_queries[:, prompt_count:], grad_pairs[:, prompt_count:].astype(jnp.bfloat16)], axis=2
    )
    grad_token_normed = jnp.einsum(
        "ihe,de->ihd", token_proj_grad, w_qkv, preferred_element_type=jnp.float32
    )
    grad_tokens = grad_middle[:, prompt_count:] + token_norm_back(grad_token_normed)[0]
    input_grad = jnp.where(kept_cols, grad_tokens, cot_seq.astype(jnp.float32))
    pair_weight = w_qkv[:, model_width:].astype(jnp.float32)
    pair_local = jnp.sum(grad_pairs[:, :prompt_count], axis=0)
    query_normed = jnp.sum(
        jnp.einsum(
            "ipe,de->ipd",
            grad_queries[:, :prompt_count],
            w_qkv[:, :model_width],
            preferred_element_type=jnp.float32,
        ),
        axis=0,
    )
    middle_sum = jnp.sum(grad_middle[:, :prompt_count], axis=0)
    prompt_local = prompt_norm_back(query_normed)[0] + middle_sum
    pair_total = lax.psum(pair_local, ("batch", "stream"))
    prompt_total = lax.psum(prompt_local, ("batch", "stream"))
    prompt_total = prompt_total + prompt_norm_back(project_pairs(pair_total, pair_weight))[0]
    penalty_weight = kept_total / (keep_mask.shape[1] * math.sqrt(total_images))
    prompt_grad = prompt_total + 2.0 * penalty_weight * prompts
    penalty = penalty_weight * jnp.sum(prompts * prompts) / (prompt_count * model_width)
    return (layer_out, prompt_out, input_grad, prompt_grad, penalty)


def solution(mesh):
    in_specs = (
        P(("batch", "stream"), None, None),
        P(),
        P(("batch", "stream"), None),
        P(("batch", "stream")),
        P(),
        P(),
        P(),
        P(),
        P(),
        P(),
        P(),
        P(),
        P(),
        P(),
        P(),
        P(),
        P(),
        P(("batch", "stream"), None, None),
        P(("batch", "stream"), None, None),
    )
    out_specs = (
        P(("batch", "stream"), None, None),
        P(("batch", "stream"), None, None),
        P(("batch", "stream"), None, None),
        P(),
        P(),
    )
    return jax.shard_map(body, mesh=mesh, in_specs=in_specs, out_specs=out_specs, check_vma=False)
```

profile of v0, /device:TPU:10, one launch (start us, length us, event | category | flops | bytes accessed | tf_op | source)
XLA Modules:
  0.0 464.4 jit_solution(8597299555711745016)
XLA Ops:
  7.2 1.6 convert_reduce_fusion
  8.8 1.8 multiply_reduce_fusion.4
  10.7 5.8 %fusion.29 = f32[4,198,2304]{2,1,0:T(8,128)S(1)} fusion(bf16[768,2304]{1,0:T(8,128)(2,1)} %param.25, f32[768]{0:T(1024)} %param.24, f32[768]{0:T(1024)} %param.23, f32[4,198]{1,0:T(4,128)S(1)} %fusion.73, f32[4,198]{1,0:T(4,128)S(1)} %broadcast_multiply_fusion.1, bf16[4,198,768]{2,0,1:T(4,128)(2,1)} %param.19), kind=kOutput, calls=%fused_computation.49 | convolution fusion | flops 2806493184 | bytes 12067008 | tf_op jit(solution)/shard_map/ihd,de->ihe/dot_general | solution.py:88
  16.5 3.0 copy-done.17
  21.0 2.8 fusion.68
  23.8 4.0 fusion.35
  27.9 1.7 copy_convert_fusion
  30.3 1.8 fusion.88
  32.1 2.7 copy.49
  35.0 2.7 pad_maximum_fusion
  37.7 2.6 copy.50
  40.3 2.6 copy.51
  42.9 5.0 %fusion.6 = (f32[4,12,248]{2,1,0:T(8,128)S(1)}, f32[4,12,248,248]{2,3,1,0:T(8,128)S(1)}) fusion(pred[4,248]{1,0:T(4,128)(4,1)S(1)} %add_compare_fusion, bf16[4,248,12,64]{1,3,2,0:T(8,128)(2,1)} %bitcast.72, bf16[4,248,12,64]{1,3,2,0:T(8,128)(2,1)} %bitcast.70), kind=kOutput, calls=%fused_computation.26 | convolution fusion | flops 386725248 | bytes 14904800 | tf_op jit(solution)/shard_map/iqhd,ikhd->ihqk/dot_general | solution.py:25
  47.9 3.4 exponential_reduce_fusion
  52.5 3.1 convolution_convert_fusion
  55.7 1.7 fusion.89
  58.8 13.1 %fusion.32 = (u8[248,3072]{1,0:T(8,128)(4,1)S(1)}, u8[248,3072]{1,0:T(8,128)(4,1)S(1)}, f32[4,248,3072]{2,1,0:T(8,128)}) fusion(f32[3072]{0:T(1024)S(1)} %copy-done.29, bf16[768,3072]{1,0:T(8,128)(2,1)S(1)} %bitcast.83, f32[4,248,768]{2,1,0:T(8,128)S(1)} %get-tuple-element.36, f32[768]{0:T(1024)S(1)} %copy-done.34, f32[768]{0:T(1024)S(1)} %copy-done.25, ...), kind=kOutput, calls=%fused_computation.60 | convolution fusion | flops 4725792768 | bytes 21505792 | tf_op jit(solution)/shard_map/ird,df->irf/dot_general | solution.py:132
  71.9 29.0 %fusion = f32[4,248,3072]{2,1,0:T(8,128)} fusion(f32[4,248,3072]{2,1,0:T(8,128)} %get-tuple-element.37, f32[3072]{0:T(1024)S(1)} %copy-done.29, u8[248,3072]{1,0:T(8,128)(4,1)S(1)} %get-tuple-element.16, u8[248,3072]{1,0:T(8,128)(4,1)S(1)} %get-tuple-element.15), kind=kLoop, calls=%fused_computation.1 | loop fusion | flops 207224832 | bytes 25915392 | tf_op jit(solution)/shard_map/jvp()/erfc | solution.py:140
  100.9 14.7 %add_add_fusion.3 = bf16[4,248,768]{2,1,0:T(8,128)(2,1)S(1)} fusion(f32[4,248,768]{2,1,0:T(8,128)S(1)} %get-tuple-element.36, bf16[3072,768]{1,0:T(8,128)(2,1)} %param.34, f32[4,248,3072]{2,1,0:T(8,128)} %fusion, f32[4,248,3072]{2,1,0:T(8,128)} %get-tuple-element.37, f32[3072]{0:T(1024)S(1)} %copy-done.29, f32[768]{0:T(1024)S(1)} %copy-done.35), kind=kOutput, calls=%fused_computation.56 | convolution fusion | flops 4695318528 | bytes 33684480 | tf_op jit(solution)/shard_map/irf,fd->ird/dot_general | solution.py:143
  115.7 2.2 broadcast_select_fusion
  117.9 19.5 %multiply_reduce_fusion.1 = (f32[4,248]{1,0:T(4,128)S(1)}, f32[4,248,768]{2,1,0:T(8,128)}) fusion(f32[4,248,768]{2,1,0:T(8,128)} %copy-done.4, f32[768]{0:T(1024)S(1)} %copy-done.25, f32[4,248]{1,0:T(4,128)S(1)} %broadcast_multiply_fusion, bf16[768,3072]{1,0:T(8,128)(2,1)} %param.32, f32[4,248,3072]{2,1,0:T(8,128)} %fusion, ...), kind=kOutput, calls=%fused_computation.55 | convolution fusion | flops 9413491712 | bytes 41458432 | tf_op jit(solution)/shard_map/irf,df->ird/dot_general | solution.py:155
  137.5 3.5 fusion.60
  142.1 2.4 add_add_fusion.2
  144.5 1.7 copy-done.9
  146.2 2.6 convolution_convert_fusion.1
  148.8 2.6 copy.56
  151.5 14.3 %multiply_reduce_fusion = (f32[4,12,248]{2,1,0:T(8,128)S(1)}, f32[4,12,248,248]{2,3,1,0:T(8,128)}) fusion(f32[4,12,248,248]{2,3,1,0:T(8,128)} %copy-done.1, f32[4,12,248]{2,1,0:T(8,128)S(1)} %log_add_fusion, pred[4,248]{1,0:T(4,128)(4,1)S(1)} %add_compare_fusion, bf16[4,248,12,64]{1,3,2,0:T(8,128)(2,1)} %bitcast.74, bf16[4,248,12,64]{1,3,2,0:T(8,128)(2,1)} %bitcast.80), kind=kOutput, calls=%fused_computation.8 | convolution fusion | flops 392629632 | bytes 26761184 | tf_op jit(solution)/shard_map/iqhd,ikhd->ihqk/dot_general | solution.py:164
  165.8 9.0 %fusion.64 = f32[4,12,64,248]{3,2,1,0:T(8,128)} fusion(bf16[4,248,12,64]{1,3,2,0:T(8,128)(2,1)S(1)} %bitcast.75, f32[4,12,248,248]{2,3,1,0:T(8,128)} %copy-done.1, f32[4,12,248]{2,1,0:T(8,128)S(1)} %log_add_fusion, pred[4,248]{1,0:T(4,128)(4,1)S(1)} %add_compare_fusion), kind=kOutput, calls=%fused_computation.121 | convolution fusion | flops 389689344 | bytes 16428512 | tf_op jit(solution)/shard_map/ihqk,iqhd->ikhd/dot_general | solution.py:167
  174.8 6.9 %multiply_convert_fusion = bf16[4,12,248,248]{2,3,1,0:T(8,128)(2,1)S(1)} fusion(f32[4,12,248,248]{2,3,1,0:T(8,128)} %get-tuple-element.41, f32[4,12,248,248]{2,3,1,0:T(8,128)S(1)} %bitcast.69, f32[4,12,248]{2,1,0:T(8,128)S(1)} %get-tuple-element.40, f32[4,12,248]{2,1,0:T(8,128)S(1)} %log_add_fusion, pred[4,248]{1,0:T(4,128)(4,1)S(1)} %add_compare_fusion), kind=kLoop, calls=%fused_computation.7 | loop fusion | flops 17713152 | bytes 29618144 | tf_op jit(solution)/shard_map/convert_element_type | solution.py:171
  181.8 3.7 convolution_multiply_fusion
  185.5 3.5 copy.61
  189.0 3.6 copy.62
  192.6 2.2 fusion.46
  195.1 4.5 fusion.13
  199.6 4.0 multiply_convert_fusion.3
  204.7 1.8 slice.87
  206.5 2.5 copy.73
  209.0 6.3 %multiply_reduce_fusion.3 = (f32[4,198]{1,0:T(4,128)S(1)}, f32[4,198,768]{2,1,0:T(8,128)S(1)}) fusion(f32[768]{0:T(1024)S(1)} %copy-done.24, f32[4,198]{1,0:T(4,128)S(1)} %broadcast_multiply_fusion.1, bf16[4,198,768]{2,0,1:T(4,128)(2,1)S(1)} %copy-done.3, bf16[768,2304]{1,0:T(8,128)(2,1)} %param.25, bf16[4,198,1536]{2,1,0:T(8,128)(2,1)} %fusion.13, ...), kind=kOutput, calls=%fused_computation.70 | convolution fusion | flops 2813183232 | bytes 10847424 | tf_op jit(solution)/shard_map/ihe,de->ihd/dot_general | solution.py:195
  217.2 2.4 fusion.33
  220.2 2.1 convolution_reduce_fusion
  222.3 41.6 %psum.23 = f32[]{:T(128)} all-reduce(f32[]{:T(128)} %convert_reduce_fusion.1), channel_id=1, replica_groups=mesh['batch'=16,'stream'=2] {'batch','stream'}, use_global_device_ids=true, to_apply=%region_23.24 | all-reduce | flops 1 | bytes 8 | tf_op jit(solution)/shard_map/psum | solution.py:65
  263.9 2.9 copy.65
  267.7 2.4 copy.67
  271.4 1.2 slice_reduce_fusion
  272.5 51.0 %all-reduce.6.cloned.1.call-done = f32[50,1536]{1,0:T(8,128)} async-done(((f32[50,1536]{1,0:T(8,128)}), f32[50,1536]{1,0:T(8,128)}) %all-reduce.6.cloned.1.call-update) | async-done | bytes 307216 | tf_op jit(solution)/shard_map/psum | solution.py:213
  323.6 4.6 multiply_reduce_fusion.5
  330.0 124.4 %all-reduce.4.cloned.1.call-done = f32[50,768]{1,0:T(8,128)} async-done(((f32[50,768]{1,0:T(8,128)}), f32[50,768]{1,0:T(8,128)}) %all-reduce.4.cloned.1.call-update) | async-done | bytes 153616 | tf_op jit(solution)/shard_map/psum | solution.py:214
  454.4 1.7 multiply_add_fusion
  (128 shorter events, 12.2 us)
Async XLA Ops:
  7.2 48.5 %copy-start = (bf16[768,768]{1,0:T(8,128)(2,1)S(1)}, bf16[768,768]{1,0:T(8,128)(2,1)}, u32[]{:S(2)}) copy-start(bf16[768,768]{1,0:T(8,128)(2,1)} %param.28) | copy-start | bytes 3538948
  7.2 316.4 %all-reduce.6.cloned.1.call-start = ((), (), s32[]{:S(2)}) async-start(), calls=%async_computation.1 | async-start | bytes 688128 | tf_op jit(solution)/shard_map/psum | solution.py:213
  10.6 10.0 %copy-start.12 = (f32[50,768]{1,0:T(8,128)S(1)}, f32[50,768]{1,0:T(8,128)}, u32[]{:S(2)}) copy-start(f32[50,768]{1,0:T(8,128)} %param.20) | copy-start | bytes 460804
  10.6 10.3 %copy-start.24 = (f32[768]{0:T(1024)S(1)}, f32[768]{0:T(1024)}, u32[]{:S(2)}) copy-start(f32[768]{0:T(1024)} %param.23) | copy-start | bytes 9220
  10.7 10.3 %copy-start.30 = (f32[768]{0:T(1024)S(1)}, f32[768]{0:T(1024)}, u32[]{:S(2)}) copy-start(f32[768]{0:T(1024)} %param.24) | copy-start | bytes 9220
  16.5 3.0 copy-start.17
  19.5 4.3 copy-start.26
  19.5 4.3 copy-start.27
  20.9 2.8 copy-start.31
  23.8 4.1 copy-start.3
  27.8 1.7 copy-start.28
  27.8 1.9 copy-start.18
  47.9 4.6 copy-start.1
  47.9 4.6 copy-start.16
  52.5 3.2 copy-start.21
  52.5 3.2 copy-start.33
  55.6 3.1 slice-start.4
  55.7 3.0 slice-start.5
  57.5 43.4 %copy-start.4 = (f32[4,248,768]{2,1,0:T(8,128)}, f32[4,248,768]{2,1,0:T(8,128)S(1)}, u32[]{:S(2)}) copy-start(f32[4,248,768]{2,1,0:T(8,128)S(1)} %get-tuple-element.36) | copy-start | bytes 9142276
  57.5 1.2 copy-start.23
  57.5 1.2 copy-start.25
  57.5 1.3 copy-start.29
  57.5 1.3 copy-start.34
  71.9 29.0 %copy-start.35 = (f32[768]{0:T(1024)S(1)}, f32[768]{0:T(1024)}, u32[]{:S(2)}) copy-start(f32[768]{0:T(1024)} %param.35) | copy-start | bytes 9220
  100.9 14.7 %copy-start.19 = (bf16[4,198,768]{2,0,1:T(4,128)(2,1)S(1)}, bf16[4,198,768]{2,0,1:T(4,128)(2,1)}, u32[]{:S(2)}) copy-start(bf16[4,198,768]{2,0,1:T(4,128)(2,1)} %param.36) | copy-start | bytes 3649540
  115.7 2.2 copy-start.22
  137.5 3.7 copy-start.5
  137.5 4.6 copy-start.11
  144.5 1.7 copy-start.9
  151.5 14.4 %copy-start.8 = (bf16[4,248,768]{1,2,0:T(8,128)(2,1)S(1)}, bf16[4,248,768]{1,2,0:T(8,128)(2,1)}, u32[]{:S(2)}) copy-start(bf16[4,248,768]{1,2,0:T(8,128)(2,1)} %copy.56) | copy-start | bytes 4571140
  151.5 23.4 %slice-start = ((s8[12189696]{0:T(1024)(128)(4,1)}), s8[4194304]{0:T(1024)(128)(4,1)S(1)}, s32[]{:S(2)}) async-start(s8[12189696]{0:T(1024)(128)(4,1)} %bitcast.68), calls=%async_computation.2 | async-start | bytes 8388608
  151.5 23.4 %slice-start.1 = ((s8[12189696]{0:T(1024)(128)(4,1)}), s8[3801088]{0:T(1024)(128)(4,1)S(1)}, s32[]{:S(2)}) async-start(s8[12189696]{0:T(1024)(128)(4,1)} %bitcast.68), calls=%async_computation.3 | async-start | bytes 7602176
  165.8 9.0 %slice-start.2 = ((s8[12189696]{0:T(1024)(128)(4,1)}), s8[4194304]{0:T(1024)(128)(4,1)S(1)}, s32[]{:S(2)}) async-start(s8[12189696]{0:T(1024)(128)(4,1)} %bitcast.68), calls=%async_computation.4 | async-start | bytes 8388608
  174.8 7.0 %copy-start.7 = (bf16[4,248,768]{1,2,0:T(8,128)(2,1)S(1)}, bf16[4,248,768]{1,2,0:T(8,128)(2,1)}, u32[]{:S(2)}) copy-start(bf16[4,248,768]{1,2,0:T(8,128)(2,1)} %copy.50) | copy-start | bytes 4571140
  181.8 3.7 copy-start.2
  194.8 259.7 %all-reduce.4.cloned.1.call-start = ((), (), s32[]{:S(2)}) async-start(), calls=%async_computation | async-start | bytes 344064 | tf_op jit(solution)/shard_map/psum | solution.py:214
  195.1 4.6 copy-start.6
  203.6 1.1 copy-start.14
  209.0 7.3 %copy-start.20 = (bf16[4,198,768]{2,0,1:T(4,128)(2,1)S(1)}, bf16[4,198,768]{2,0,1:T(4,128)(2,1)}, u32[]{:S(2)}) copy-start(bf16[4,198,768]{2,0,1:T(4,128)(2,1)} %param.36) | copy-start | bytes 3649540
  215.3 1.9 copy-start.10
  217.2 2.4 copy-start.36
  217.2 3.0 copy-start.15
  220.2 46.6 %slice-start.3 = ((bf16[4,248,768]{2,1,0:T(8,128)(2,1)}), bf16[4,50,768]{2,1,0:T(8,128)(2,1)S(1)}, s32[]{:S(2)}) async-start(bf16[4,248,768]{2,1,0:T(8,128)(2,1)} %copy-done.22), calls=%async_computation.5 | async-start | bytes 688128 | tf_op jit(solution)/shard_map/slice | solution.py:148
  263.9 3.8 copy-start.13
  270.1 58.1 %copy-start.32 = (f32[50]{0:T(128)S(1)}, f32[50]{0:T(128)}, u32[]{:S(2)}) copy-start(f32[50]{0:T(128)} %copy-done.31) | copy-start | bytes 604
Sparse Core Ops, SparseCore 0:
  194.9 128.5 all-reduce.5
  330.6 123.8 all-reduce.3
where the time goes:
time: 470 us; the launch traced here: 464 us
  waiting for transfers between devices  175 us (37%)
  matrix products  112 us (24%)
  other arithmetic  75.7 us (16%)
  blocking collectives  41.6 us (9%)
  local copies, waits for them, and re-layouts  41.1 us (9%)
  between operations  17.9 us (4%)
    psum x1, waiting for transfers between devices, body(): prompt_total = lax.psum(prompt_local, ('batch', 'stream'))  124 us
    psum x1, waiting for transfers between devices, body(): pair_total = lax.psum(pair_local, ('batch', 'stream'))  51 us
    psum x1, blocking collectives, body(): kept_total = lax.psum(count_sum, ('batch', 'stream'))  41.6 us
    another operation x1, other arithmetic, body(): jax.nn.gelu(rows_in, approximate=False)  29 us
    dot_general x1, matrix products, body(): jnp.einsum('irf,df->ird', grad_hidden, w_fc1, preferred_element_type=jnp....  19.5 us
    unnamed x89, local copies, waits for them, and re-layouts  18.5 us
    dot_general x1, matrix products, body(): jnp.einsum('irf,fd->ird', activated.astype(jnp.bfloat16), w_fc2, preferre...  14.7 us
    dot_general x1, matrix products, body(): jnp.einsum('iqhd,ikhd->ihqk', context_heads, value_heads, preferred_eleme...  14.3 us
  transfers between devices with their start and end apart: 2, of which 2 were waited for; matrix products, arithmetic and copies ran while one was open for 7% of the time, Pallas kernels for 0%

commit v1 on v0

--- a/solution.py
+++ b/solution.py
@@ -210,7 +210,7 @@
     )
     middle_sum = jnp.sum(grad_middle[:, :prompt_count], axis=0)
     prompt_local = prompt_norm_back(query_normed)[0] + middle_sum
-    pair_total = lax.psum(pair_local, ("batch", "stream"))
+    pair_total = lax.psum(lax.psum(pair_local, "stream"), "batch")
     prompt_total = lax.psum(prompt_local, ("batch", "stream"))
     prompt_total = prompt_total + prompt_norm_back(project_pairs(pair_total, pair_weight))[0]
     penalty_weight = kept_total / (keep_mask.shape[1] * math.sqrt(total_images))

time: 470 us -> 475 us (1.011)
  waiting for transfers between devices: 175 us -> 181 us
    psum x1 -> x2, waiting for transfers between devices: 51 us -> 55.8 us  [body(): pair_total = lax.psum(lax.psum(pair_local, 'stream'), 'batch')]
    unnamed x89 -> x87, local copies, waits for them, and re-layouts: 18.5 us -> 18.5 us
  transfers between devices with their start and end apart: 2 -> 3, of which waited for: 2 -> 2; matrix products, arithmetic and copies ran while one was open for 7% -> 7% of each run, Pallas kernels for 0% -> 0%
where the time goes in v1:
time: 475 us; the launch traced here: 470 us
  waiting for transfers between devices  181 us (38%)
  matrix products  113 us (24%)
  other arithmetic  75.7 us (16%)
  blocking collectives  41.7 us (9%)
  local copies, waits for them, and re-layouts  41 us (9%)
  between operations  17.7 us (4%)
    psum x1, waiting for transfers between devices, body(): prompt_total = lax.psum(prompt_local, ('batch', 'stream'))  125 us
    psum x2, waiting for transfers between devices, body(): pair_total = lax.psum(lax.psum(pair_local, 'stream'), 'batch')  55.8 us
    psum x1, blocking collectives, body(): kept_total = lax.psum(count_sum, ('batch', 'stream'))  41.7 us
    another operation x1, other arithmetic, body(): jax.nn.gelu(rows_in, approximate=False)  29 us
    dot_general x1, matrix products, body(): jnp.einsum('irf,df->ird', grad_hidden, w_fc1, preferred_element_type=jnp....  19.5 us
    unnamed x87, local copies, waits for them, and re-layouts  18.5 us
    dot_general x1, matrix products, body(): jnp.einsum('irf,fd->ird', activated.astype(jnp.bfloat16), w_fc2, preferre...  14.7 us
    dot_general x1, matrix products, body(): jnp.einsum('iqhd,ikhd->ihqk', context_heads, value_heads, preferred_eleme...  14.3 us
  transfers between devices with their start and end apart: 3, of which 2 were waited for; matrix products, arithmetic and copies ran while one was open for 7% of the time, Pallas kernels for 0%

profile of v1, /device:TPU:10, one launch (start us, length us, event | category | flops | bytes accessed | tf_op | source)
XLA Modules:
  0.0 469.9 jit_solution(3961500707316778298)
XLA Ops:
  7.2 1.6 convert_reduce_fusion
  8.8 1.8 multiply_reduce_fusion.4
  10.7 5.8 %fusion.29 = f32[4,198,2304]{2,1,0:T(8,128)S(1)} fusion(bf16[768,2304]{1,0:T(8,128)(2,1)} %param.25, f32[768]{0:T(1024)} %param.24, f32[768]{0:T(1024)} %param.23, f32[4,198]{1,0:T(4,128)S(1)} %fusion.73, f32[4,198]{1,0:T(4,128)S(1)} %broadcast_multiply_fusion.1, bf16[4,198,768]{2,0,1:T(4,128)(2,1)} %param.19), kind=kOutput, calls=%fused_computation.49 | convolution fusion | flops 2806493184 | bytes 12067008 | tf_op jit(solution)/shard_map/ihd,de->ihe/dot_general | solution.py:88
  16.5 3.0 copy-done.16
  21.0 2.8 fusion.68
  23.8 4.0 fusion.35
  27.9 1.7 copy_convert_fusion
  30.3 1.8 fusion.88
  32.1 2.7 copy.49
  35.0 2.7 pad_maximum_fusion
  37.7 2.6 copy.50
  40.3 2.6 copy.51
  42.9 5.0 %fusion.6 = (f32[4,12,248]{2,1,0:T(8,128)S(1)}, f32[4,12,248,248]{2,3,1,0:T(8,128)S(1)}) fusion(pred[4,248]{1,0:T(4,128)(4,1)S(1)} %add_compare_fusion, bf16[4,248,12,64]{1,3,2,0:T(8,128)(2,1)} %bitcast.72, bf16[4,248,12,64]{1,3,2,0:T(8,128)(2,1)} %bitcast.70), kind=kOutput, calls=%fused_computation.26 | convolution fusion | flops 386725248 | bytes 14904800 | tf_op jit(solution)/shard_map/iqhd,ikhd->ihqk/dot_general | solution.py:25
  47.9 3.4 exponential_reduce_fusion
  52.5 3.1 convolution_convert_fusion
  55.7 1.7 fusion.89
  58.8 13.1 %fusion.32 = (u8[248,3072]{1,0:T(8,128)(4,1)S(1)}, u8[248,3072]{1,0:T(8,128)(4,1)S(1)}, f32[4,248,3072]{2,1,0:T(8,128)}) fusion(f32[3072]{0:T(1024)S(1)} %copy-done.28, bf16[768,3072]{1,0:T(8,128)(2,1)S(1)} %bitcast.83, f32[4,248,768]{2,1,0:T(8,128)S(1)} %get-tuple-element.36, f32[768]{0:T(1024)S(1)} %copy-done.33, f32[768]{0:T(1024)S(1)} %copy-done.24, ...), kind=kOutput, calls=%fused_computation.60 | convolution fusion | flops 4725792768 | bytes 21505792 | tf_op jit(solution)/shard_map/ird,df->irf/dot_general | solution.py:132
  71.9 29.0 %fusion = f32[4,248,3072]{2,1,0:T(8,128)} fusion(f32[4,248,3072]{2,1,0:T(8,128)} %get-tuple-element.37, f32[3072]{0:T(1024)S(1)} %copy-done.28, u8[248,3072]{1,0:T(8,128)(4,1)S(1)} %get-tuple-element.16, u8[248,3072]{1,0:T(8,128)(4,1)S(1)} %get-tuple-element.15), kind=kLoop, calls=%fused_computation.1 | loop fusion | flops 207224832 | bytes 25915392 | tf_op jit(solution)/shard_map/jvp()/erfc | solution.py:140
  100.9 14.7 %add_add_fusion.3 = bf16[4,248,768]{2,1,0:T(8,128)(2,1)S(1)} fusion(f32[4,248,768]{2,1,0:T(8,128)S(1)} %get-tuple-element.36, bf16[3072,768]{1,0:T(8,128)(2,1)} %param.34, f32[4,248,3072]{2,1,0:T(8,128)} %fusion, f32[4,248,3072]{2,1,0:T(8,128)} %get-tuple-element.37, f32[3072]{0:T(1024)S(1)} %copy-done.28, f32[768]{0:T(1024)S(1)} %copy-done.34), kind=kOutput, calls=%fused_computation.56 | convolution fusion | flops 4695318528 | bytes 33684480 | tf_op jit(solution)/shard_map/irf,fd->ird/dot_general | solution.py:143
  115.7 2.2 broadcast_select_fusion
  117.9 19.5 %multiply_reduce_fusion.1 = (f32[4,248]{1,0:T(4,128)S(1)}, f32[4,248,768]{2,1,0:T(8,128)}) fusion(f32[4,248,768]{2,1,0:T(8,128)} %copy-done.4, f32[768]{0:T(1024)S(1)} %copy-done.24, f32[4,248]{1,0:T(4,128)S(1)} %broadcast_multiply_fusion, bf16[768,3072]{1,0:T(8,128)(2,1)} %param.32, f32[4,248,3072]{2,1,0:T(8,128)} %fusion, ...), kind=kOutput, calls=%fused_computation.55 | convolution fusion | flops 9413491712 | bytes 41458432 | tf_op jit(solution)/shard_map/irf,df->ird/dot_general | solution.py:155
  137.5 3.5 fusion.60
  142.1 2.4 add_add_fusion.2
  144.5 1.7 copy-done.9
  146.2 2.6 convolution_convert_fusion.1
  148.8 2.6 copy.56
  151.5 14.3 %multiply_reduce_fusion = (f32[4,12,248]{2,1,0:T(8,128)S(1)}, f32[4,12,248,248]{2,3,1,0:T(8,128)}) fusion(f32[4,12,248,248]{2,3,1,0:T(8,128)} %copy-done.1, f32[4,12,248]{2,1,0:T(8,128)S(1)} %log_add_fusion, pred[4,248]{1,0:T(4,128)(4,1)S(1)} %add_compare_fusion, bf16[4,248,12,64]{1,3,2,0:T(8,128)(2,1)} %bitcast.74, bf16[4,248,12,64]{1,3,2,0:T(8,128)(2,1)} %bitcast.80), kind=kOutput, calls=%fused_computation.8 | convolution fusion | flops 392629632 | bytes 26761184 | tf_op jit(solution)/shard_map/iqhd,ikhd->ihqk/dot_general | solution.py:164
  165.8 9.0 %fusion.64 = f32[4,12,64,248]{3,2,1,0:T(8,128)} fusion(bf16[4,248,12,64]{1,3,2,0:T(8,128)(2,1)S(1)} %bitcast.75, f32[4,12,248,248]{2,3,1,0:T(8,128)} %copy-done.1, f32[4,12,248]{2,1,0:T(8,128)S(1)} %log_add_fusion, pred[4,248]{1,0:T(4,128)(4,1)S(1)} %add_compare_fusion), kind=kOutput, calls=%fused_computation.121 | convolution fusion | flops 389689344 | bytes 16428512 | tf_op jit(solution)/shard_map/ihqk,iqhd->ikhd/dot_general | solution.py:167
  174.8 6.9 %multiply_convert_fusion = bf16[4,12,248,248]{2,3,1,0:T(8,128)(2,1)S(1)} fusion(f32[4,12,248,248]{2,3,1,0:T(8,128)} %get-tuple-element.41, f32[4,12,248,248]{2,3,1,0:T(8,128)S(1)} %bitcast.69, f32[4,12,248]{2,1,0:T(8,128)S(1)} %get-tuple-element.40, f32[4,12,248]{2,1,0:T(8,128)S(1)} %log_add_fusion, pred[4,248]{1,0:T(4,128)(4,1)S(1)} %add_compare_fusion), kind=kLoop, calls=%fused_computation.7 | loop fusion | flops 17713152 | bytes 29618144 | tf_op jit(solution)/shard_map/convert_element_type | solution.py:171
  181.8 3.7 convolution_multiply_fusion
  185.5 3.5 copy.61
  189.0 3.6 copy.62
  192.6 2.1 fusion.46
  195.1 4.5 fusion.13
  199.6 3.9 multiply_convert_fusion.3
  204.7 1.8 slice.87
  206.5 2.5 copy.73
  209.0 6.3 %multiply_reduce_fusion.3 = (f32[4,198]{1,0:T(4,128)S(1)}, f32[4,198,768]{2,1,0:T(8,128)S(1)}) fusion(f32[768]{0:T(1024)S(1)} %copy-done.23, f32[4,198]{1,0:T(4,128)S(1)} %broadcast_multiply_fusion.1, bf16[4,198,768]{2,0,1:T(4,128)(2,1)S(1)} %copy-done.3, bf16[768,2304]{1,0:T(8,128)(2,1)} %param.25, bf16[4,198,1536]{2,1,0:T(8,128)(2,1)} %fusion.13, ...), kind=kOutput, calls=%fused_computation.70 | convolution fusion | flops 2813183232 | bytes 10847424 | tf_op jit(solution)/shard_map/ihe,de->ihd/dot_general | solution.py:195
  217.2 2.4 fusion.33
  220.3 1.2 slice_reduce_fusion
  221.4 41.7 %psum.31 = f32[]{:T(128)} all-reduce(f32[]{:T(128)} %convert_reduce_fusion.1), channel_id=1, replica_groups=mesh['batch'=16,'stream'=2] {'batch','stream'}, use_global_device_ids=true, to_apply=%region_24.25 | all-reduce | flops 1 | bytes 8 | tf_op jit(solution)/shard_map/psum | solution.py:65
  263.1 2.9 copy.65
  266.9 2.4 copy.67
  270.5 2.3 convolution_reduce_fusion
  272.9 55.8 %all-reduce.9.cloned.1.call-done = f32[50,1536]{1,0:T(8,128)} async-done(((f32[50,1536]{1,0:T(8,128)}), f32[50,1536]{1,0:T(8,128)}) %all-reduce.9.cloned.1.call-update) | async-done | bytes 307216 | tf_op jit(solution)/shard_map/psum | solution.py:213
  328.7 4.6 multiply_reduce_fusion.5
  335.2 125.1 %all-reduce.5.cloned.1.call-done = f32[50,768]{1,0:T(8,128)} async-done(((f32[50,768]{1,0:T(8,128)}), f32[50,768]{1,0:T(8,128)}) %all-reduce.5.cloned.1.call-update) | async-done | bytes 153616 | tf_op jit(solution)/shard_map/psum | solution.py:214
  460.3 1.7 multiply_add_fusion
  (129 shorter events, 12.2 us)
Async XLA Ops:
  7.2 48.5 %copy-start = (bf16[768,768]{1,0:T(8,128)(2,1)S(1)}, bf16[768,768]{1,0:T(8,128)(2,1)}, u32[]{:S(2)}) copy-start(bf16[768,768]{1,0:T(8,128)(2,1)} %param.28) | copy-start | bytes 3538948
  7.2 213.0 %all-reduce.7.cloned.1.call-start = ((), (), s32[]{:S(2)}) async-start(), calls=%async_computation.1 | async-start | bytes 688128 | tf_op jit(solution)/shard_map/psum | solution.py:213
  10.6 10.0 %copy-start.12 = (f32[50,768]{1,0:T(8,128)S(1)}, f32[50,768]{1,0:T(8,128)}, u32[]{:S(2)}) copy-start(f32[50,768]{1,0:T(8,128)} %param.20) | copy-start | bytes 460804
  10.6 10.3 %copy-start.23 = (f32[768]{0:T(1024)S(1)}, f32[768]{0:T(1024)}, u32[]{:S(2)}) copy-start(f32[768]{0:T(1024)} %param.23) | copy-start | bytes 9220
  10.7 10.3 %copy-start.29 = (f32[768]{0:T(1024)S(1)}, f32[768]{0:T(1024)}, u32[]{:S(2)}) copy-start(f32[768]{0:T(1024)} %param.24) | copy-start | bytes 9220
  16.5 3.0 copy-start.16
  19.4 4.3 copy-start.25
  19.5 4.3 copy-start.26
  20.9 2.8 copy-start.30
  23.8 4.1 copy-start.3
  27.8 1.7 copy-start.27
  27.8 1.9 copy-start.17
  47.9 4.6 copy-start.1
  47.9 4.6 copy-start.15
  52.5 3.2 copy-start.20
  52.5 3.2 copy-start.32
  55.6 3.1 slice-start.4
  55.7 3.0 slice-start.5
  57.5 43.4 %copy-start.4 = (f32[4,248,768]{2,1,0:T(8,128)}, f32[4,248,768]{2,1,0:T(8,128)S(1)}, u32[]{:S(2)}) copy-start(f32[4,248,768]{2,1,0:T(8,128)S(1)} %get-tuple-element.36) | copy-start | bytes 9142276
  57.5 1.2 copy-start.22
  57.5 1.2 copy-start.24
  57.5 1.3 copy-start.28
  57.5 1.3 copy-start.33
  71.9 29.0 %copy-start.34 = (f32[768]{0:T(1024)S(1)}, f32[768]{0:T(1024)}, u32[]{:S(2)}) copy-start(f32[768]{0:T(1024)} %param.35) | copy-start | bytes 9220
  100.9 14.7 %copy-start.18 = (bf16[4,198,768]{2,0,1:T(4,128)(2,1)S(1)}, bf16[4,198,768]{2,0,1:T(4,128)(2,1)}, u32[]{:S(2)}) copy-start(bf16[4,198,768]{2,0,1:T(4,128)(2,1)} %param.36) | copy-start | bytes 3649540
  115.7 2.2 copy-start.21
  137.5 3.7 copy-start.5
  137.5 4.6 copy-start.11
  144.5 1.7 copy-start.9
  151.5 14.4 %copy-start.8 = (bf16[4,248,768]{1,2,0:T(8,128)(2,1)S(1)}, bf16[4,248,768]{1,2,0:T(8,128)(2,1)}, u32[]{:S(2)}) copy-start(bf16[4,248,768]{1,2,0:T(8,128)(2,1)} %copy.56) | copy-start | bytes 4571140
  151.5 23.4 %slice-start = ((s8[12189696]{0:T(1024)(128)(4,1)}), s8[4194304]{0:T(1024)(128)(4,1)S(1)}, s32[]{:S(2)}) async-start(s8[12189696]{0:T(1024)(128)(4,1)} %bitcast.68), calls=%async_computation.3 | async-start | bytes 8388608
  151.5 23.4 %slice-start.1 = ((s8[12189696]{0:T(1024)(128)(4,1)}), s8[3801088]{0:T(1024)(128)(4,1)S(1)}, s32[]{:S(2)}) async-start(s8[12189696]{0:T(1024)(128)(4,1)} %bitcast.68), calls=%async_computation.4 | async-start | bytes 7602176
  165.8 9.0 %slice-start.2 = ((s8[12189696]{0:T(1024)(128)(4,1)}), s8[4194304]{0:T(1024)(128)(4,1)S(1)}, s32[]{:S(2)}) async-start(s8[12189696]{0:T(1024)(128)(4,1)} %bitcast.68), calls=%async_computation.5 | async-start | bytes 8388608
  174.8 7.0 %copy-start.7 = (bf16[4,248,768]{1,2,0:T(8,128)(2,1)S(1)}, bf16[4,248,768]{1,2,0:T(8,128)(2,1)}, u32[]{:S(2)}) copy-start(bf16[4,248,768]{1,2,0:T(8,128)(2,1)} %copy.50) | copy-start | bytes 4571140
  181.8 3.7 copy-start.2
  194.8 133.9 %all-reduce.9.cloned.1.call-start = ((), (), s32[]{:S(2)}) async-start(), calls=%async_computation.2 | async-start | bytes 688128 | tf_op jit(solution)/shard_map/psum | solution.py:213
  195.0 4.6 copy-start.6
  203.5 1.1 copy-start.14
  209.0 7.4 %copy-start.19 = (bf16[4,198,768]{2,0,1:T(4,128)(2,1)S(1)}, bf16[4,198,768]{2,0,1:T(4,128)(2,1)}, u32[]{:S(2)}) copy-start(bf16[4,198,768]{2,0,1:T(4,128)(2,1)} %param.36) | copy-start | bytes 3649540
  215.3 1.9 copy-start.10
  217.2 2.4 copy-start.35
  219.6 46.4 %slice-start.3 = ((bf16[4,248,768]{2,1,0:T(8,128)(2,1)}), bf16[4,50,768]{2,1,0:T(8,128)(2,1)S(1)}, s32[]{:S(2)}) async-start(bf16[4,248,768]{2,1,0:T(8,128)(2,1)} %copy-done.21), calls=%async_computation.6 | async-start | bytes 688128 | tf_op jit(solution)/shard_map/slice | solution.py:148
  220.2 240.0 %all-reduce.5.cloned.1.call-start = ((), (), s32[]{:S(2)}) async-start(), calls=%async_computation | async-start | bytes 344064 | tf_op jit(solution)/shard_map/psum | solution.py:214
  263.1 3.8 copy-start.13
  269.2 64.0 %copy-start.31 = (f32[50]{0:T(128)S(1)}, f32[50]{0:T(128)}, u32[]{:S(2)}) copy-start(f32[50]{0:T(128)} %copy-done.30) | copy-start | bytes 604
Sparse Core Ops, SparseCore 0:
  194.9 19.7 all-reduce.6
  220.3 108.2 all-reduce.8
  335.7 124.5 all-reduce.4
